TPU v7x, 512 devices: a whole 4x8x8 slice. The times are simulated.
512 devices in a mesh: chan: 32 (over z, y_hi), seg: 16 (over x, y_lo, core).
Axes of the slice: x: 4, y: 8 (y_hi: 4, y_lo: 2; y = y_hi * 2 + y_lo), z: 8, core: 2. Of those that a mesh axis runs over, the one named last changes fastest.
Arguments:
- strain: float32 [1024, 40000], P('chan', 'seg')
- source_channels: int32 [32], replicated, may hold values from 0 to 1023, as said below
Outputs:
- stack: float32 [32, 1024, 501], P('seg', 'chan')
Inputs may be any that keep to these rules, and one draw needn't show every extreme that they name: `source_channels`: distinct channels; channel 0 and channel 1024 - 1 are always among them.
All inputs are finite; a program needn't handle non-finite values.
Results may differ from a plain program's by a relative error of at most 0.0001.
Values sent between devices are 32-bit elements; how exact they have to be, the bound alone decides.
A program may use at most 64 MiB of HBM per device.

v0:
```python
import math
import jax
import jax.numpy as jnp
from jax import lax
from jax.sharding import PartitionSpec as P

SEG_LEN = 625
TAPS = 63
MAXLAG = 250
cutoff = 0.1
water_level = 0.5
epsilon = 1e-06
block_width = 128


def from_behind(value, axis, steps):
    count = lax.axis_size(axis)
    leading, last = (max(0, -steps), min(count, count - steps))
    return lax.ppermute(value, axis, [(source, source + steps) for source in range(leading, last)])


def tap_shape(position, count):
    window = 0.54 - 0.46 * jnp.cos(2.0 * math.pi * position / (count - 1))
    return window * 2.0 * cutoff * jnp.sinc(2.0 * cutoff * (position - (count - 1) / 2.0))


def band_table(count):
    total = jnp.sum(tap_shape(jnp.arange(count).astype(jnp.float32), count))
    span = 5 * block_width
    offsets = jnp.arange(span)[:, None] - 4 * jnp.arange(block_width)[None, :]
    valid = (offsets >= 0) & (offsets <= count - 1)
    values = tap_shape((count - 1 - offsets).astype(jnp.float32), count) / total
    return jnp.where(valid, values, 0.0)


def decimate(extended, seg_len):
    channel_count = extended.shape[0]
    blocks = -(-seg_len // block_width)
    span = 5 * block_width
    stride = 4 * block_width
    needed = stride * (blocks - 1) + span
    extended = jnp.pad(extended, ((0, 0), (0, needed - extended.shape[1])))
    windows = jnp.stack(
        [
            extended[:, stride * block_index : stride * block_index + span]
            for block_index in range(blocks)
        ],
        axis=1,
    )
    outputs = jnp.einsum("rbi,im->rbm", windows, band_table(TAPS), precision=lax.Precision.HIGHEST)
    return outputs.reshape(channel_count, blocks * block_width)[:, :seg_len]


def forward_table(seg_len, block_index):
    samples = jnp.arange(seg_len)[:, None]
    freqs = block_index * block_width + jnp.arange(block_width)[None, :]
    phase = jnp.mod(samples * freqs, 2 * seg_len).astype(jnp.float32) * (math.pi / seg_len)
    valid = freqs <= seg_len
    return jnp.concatenate(
        [jnp.where(valid, jnp.cos(phase), 0.0), jnp.where(valid, -jnp.sin(phase), 0.0)], axis=1
    )


def inverse_table(block_index, factor):
    freqs = block_index * block_width + jnp.arange(block_width)[:, None]
    lag_values = jnp.arange(2 * MAXLAG + 1)[None, :] - MAXLAG
    phase = jnp.mod(freqs * lag_values, 2 * SEG_LEN).astype(jnp.float32) * (math.pi / SEG_LEN)
    weight = jnp.where((freqs == 0) | (freqs == SEG_LEN), 1.0, 2.0) * factor
    weight = jnp.where(freqs <= SEG_LEN, weight, 0.0)
    return jnp.concatenate([weight * jnp.cos(phase), -weight * jnp.sin(phase)], axis=0)


def whiten(real_part, imag_part, seg_len):
    power = real_part * real_part + imag_part * imag_part
    bin_span = power.shape[1]
    padded = jnp.pad(power, ((0, 0), (2, 2)))
    smooth = (
        padded[:, 0:bin_span]
        + padded[:, 1 : bin_span + 1]
        + padded[:, 2 : bin_span + 2]
        + padded[:, 3 : bin_span + 3]
        + padded[:, 4 : bin_span + 4]
    ) / 5.0
    floor_level = water_level * (jnp.sum(power, axis=1, keepdims=True) / (seg_len + 1))
    inverse_norm = 1.0 / jnp.sqrt(jnp.maximum(smooth, floor_level) + epsilon)
    return (real_part * inverse_norm, imag_part * inverse_norm)


def whitened_spectra(traces):
    seg_len = traces.shape[1]
    blocks = (seg_len + block_width) // block_width
    real_parts = []
    imag_parts = []
    for block_index in range(blocks):
        product = jnp.dot(
            traces,
            forward_table(seg_len, block_index),
            precision=lax.Precision.HIGHEST,
            preferred_element_type=jnp.float32,
        )
        real_parts.append(product[:, :block_width])
        imag_parts.append(product[:, block_width:])
    real_part, imag_part = whiten(
        jnp.concatenate(real_parts, 1), jnp.concatenate(imag_parts, 1), seg_len
    )
    return jnp.stack([real_part, imag_part], axis=1)


def back_block(cross_re, cross_im, block_index, factor):
    joined = jnp.concatenate([cross_re, cross_im], axis=2)
    return jnp.einsum(
        "sck,kl->scl", joined, inverse_table(block_index, factor), precision=lax.Precision.HIGHEST
    )


def correlate(sources, channels, factor):
    blocks = sources.shape[2] // block_width
    total = jnp.zeros((sources.shape[0], channels.shape[0], 2 * MAXLAG + 1), jnp.float32)
    for block_index in range(blocks):
        first_bin = block_index * block_width
        src_re = sources[:, 0, first_bin : first_bin + block_width]
        src_im = sources[:, 1, first_bin : first_bin + block_width]
        chan_re = channels[:, 0, first_bin : first_bin + block_width]
        chan_im = channels[:, 1, first_bin : first_bin + block_width]
        cross_re = (
            src_re[:, None, :] * chan_re[None, :, :] + src_im[:, None, :] * chan_im[None, :, :]
        )
        cross_im = (
            src_re[:, None, :] * chan_im[None, :, :] - src_im[:, None, :] * chan_re[None, :, :]
        )
        total = total + back_block(cross_re, cross_im, block_index, factor)
    return total


def collect_sources(chan_spec, picked_index, inside):
    picked = jnp.where(inside[:, None, None], jnp.take(chan_spec, picked_index, axis=0), 0.0)
    return lax.psum(picked, "chan")


def body(strain, source_channels):
    channel_count = strain.shape[0]
    margin = TAPS - 3
    last_samples = strain[:, strain.shape[1] - margin :]
    before = from_behind(last_samples, "seg", 1)
    extended = jnp.concatenate([before, strain], axis=1)
    traces = decimate(extended, SEG_LEN)
    segments = lax.axis_size("seg")
    factor = 1.0 / math.sqrt(2.0 * SEG_LEN * segments)
    base = lax.axis_index("chan") * channel_count
    local = source_channels - base
    inside = (local >= 0) & (local < channel_count)
    picked_index = jnp.clip(local, 0, channel_count - 1)
    chan_spec = whitened_spectra(traces)
    collected = collect_sources(chan_spec, picked_index, inside)
    return lax.psum_scatter(
        correlate(collected, chan_spec, factor), "seg", scatter_dimension=0, tiled=True
    )


def solution(mesh):
    in_specs = (P("chan", "seg"), P())
    out_specs = P("seg", "chan", None)
    return jax.shard_map(body, mesh=mesh, in_specs=in_specs, out_specs=out_specs, check_vma=False)
```

profile of v0, /device:TPU:16, one launch (start us, length us, event | category | flops | bytes accessed | tf_op | source)
XLA Modules:
  0.0 421.2 jit_solution(7290643064510937001)
XLA Ops:
  6.5 0.8 slice.131
  7.3 1.7 collective-permute-start
  9.3 0.7 compare_and_fusion
  9.9 1.4 cosine_select_fusion.4
  11.3 1.4 cosine_select_fusion
  12.6 1.4 cosine_select_fusion.1
  14.0 1.4 cosine_select_fusion.2
  15.4 1.4 cosine_select_fusion.3
  16.7 5.5 %cosine_multiply_fusion = (f32[128,501]{0,1:T(8,128)S(1)}, f32[128,501]{0,1:T(8,128)S(1)}, f32[128,501]{0,1:T(8,128)S(1)}, f32[128,501]{0,1:T(8,128)S(1)}, f32[1...) fusion(s32[128]{0:T(128)S(1)} %iota_add_fusion.1, ...), kind=kLoop, calls=%fused_computation.165 | loop fusion | flops 3527040 | bytes 2574292 | tf_op jit(solution)/shard_map/mul | solution.py:70
  22.2 0.7 fusion.176
  23.3 0.1 pad_maximum_fusion
  23.4 2.8 convolution_bitcast_fusion
  26.2 0.4 fusion.19
  26.7 0.4 fusion.35
  27.1 0.4 fusion.31
  27.5 0.4 fusion.27
  28.0 0.4 fusion.23
  28.6 0.2 multiply_bitcast_fusion.1
  28.8 0.1 copy.4
  28.9 0.7 gather_fusion
  29.7 0.8 select_select_fusion
  30.6 306.1 %all-reduce.4.cloned.1.call-done = f32[32,2,640]{2,1,0:T(2,128)} async-done(((f32[32,2,640]{2,1,0:T(2,128)}), f32[32,2,640]{2,1,0:T(2,128)}) %all-reduce.4.cloned.1.call-update) | async-done | bytes 163856 | tf_op jit(solution)/shard_map/psum | solution.py:137
  336.7 1.1 fusion.212
  337.8 0.1 multiply_add_fusion.4
  337.9 1.9 fusion
  339.8 0.2 multiply_add_fusion
  340.0 1.9 fusion.12
  341.9 0.3 multiply_add_fusion.2
  342.2 1.9 fusion.8
  344.1 1.9 fusion.4
  346.0 3.7 add_add_fusion
  349.7 64.7 %reduce-scatter.2.cloned.1.call-done = f32[2,32,501]{2,1,0:T(8,128)} async-done(((f32[32,32,501]{2,1,0:T(8,128)}), f32[2,32,501]{2,1,0:T(8,128)}) %reduce-scatter.2.cloned.1.call-update) | async-done | bytes 128272 | tf_op jit(solution)/shard_map/reduce_scatter | solution.py:155
  (41 shorter events, 0.7 us)
Async XLA Ops:
  6.5 330.2 %all-reduce.4.cloned.1.call-start = ((), (), s32[]{:S(2)}) async-start(), calls=%async_computation.1 | async-start | bytes 327680 | tf_op jit(solution)/shard_map/psum | solution.py:137
  7.3 15.6 %collective-permute-start = (f32[32,60]{1,0:T(8,128)S(1)}, f32[32,60]{1,0:T(8,128)S(1)}, u32[]{:S(2)}, u32[]{:S(2)}) collective-permute-start(f32[32,60]{1,0:T(8,128)S(1)} %slice.131), channel_id=1, source_target_pairs={{0,1},{1,2},{2,3},{3,4},{4,5},{5,6},{6,7},{7,8},{8,9},{9,10},{10,1... | collective-permute-start | bytes 23048 | tf_op jit(solution)/shard_map/ppermute | solution.py:19
  14.0 8.9 %copy-start = (f32[32,2500]{1,0:T(8,128)S(1)}, f32[32,2500]{1,0:T(8,128)}, u32[]{:S(2)}) copy-start(f32[32,2500]{1,0:T(8,128)} %param.2) | copy-start | bytes 960004
  30.5 383.8 %reduce-scatter.2.cloned.1.call-start = ((), (), s32[]{:S(2)}) async-start(), calls=%async_computation.2 | async-start | bytes 2228224 | tf_op jit(solution)/shard_map/reduce_scatter | solution.py:155
Sparse Core Ops, SparseCore 0:
  30.7 305.9 all-reduce.3
  349.8 64.5 reduce-scatter.1
where the time goes:
time: 421 us
  waiting for transfers between devices  371 us (88%)
  matrix products  16 us (4%)
  other arithmetic  15.7 us (4%)
  between operations  13.8 us (3%)
    psum x1, waiting for transfers between devices, collect_sources(): return lax.psum(picked, 'chan')  306 us
    reduce_scatter x1, waiting for transfers between devices, body(): lax.psum_scatter(correlate(collected, chan_spec, factor), 'seg', scatter_...  64.7 us
    dot_general x5, matrix products, back_block(): jnp.einsum('sck,kl->scl', joined, inverse_table(block_index, factor), pre...  11.2 us
  transfers between devices with their start and end apart: 3, of which 2 were waited for; matrix products, arithmetic and copies ran while one was open for 3% of the time, Pallas kernels for 0%

commit v1 on v0

--- a/solution.py
+++ b/solution.py
@@ -134,7 +134,7 @@
 
 def collect_sources(chan_spec, picked_index, inside):
     picked = jnp.where(inside[:, None, None], jnp.take(chan_spec, picked_index, axis=0), 0.0)
-    return lax.psum(picked, "chan")
+    return jnp.sum(lax.all_gather(picked, "chan"), axis=0)
 
 
 def body(strain, source_channels):

time: 421 us -> 230 us (0.55)
  waiting for transfers between devices: 371 us -> 177 us
    psum x1 -> x0, waiting for transfers between devices: 306 us -> none  [collect_sources(): return lax.psum(picked, 'chan')]
    all_gather x0 -> x1, waiting for transfers between devices: none -> 107 us  [collect_sources(): return jnp.sum(lax.all_gather(picked, 'chan'), axis=0)]
    reduce_scatter x1, waiting for transfers between devices: 64.7 us -> 69.6 us  [body(): lax.psum_scatter(correlate(collected, chan_spec, factor), 'seg', scatter_...]
  transfers between devices with their start and end apart: 3 -> 3, of which waited for: 2 -> 2; matrix products, arithmetic and copies ran while one was open for 3% -> 6% of each run, Pallas kernels for 0% -> 0%
where the time goes in v1:
time: 230 us; the launch traced here: 229 us
  waiting for transfers between devices  177 us (77%)
  other arithmetic  17.8 us (8%)
  matrix products  16.3 us (7%)
  between operations  13.8 us (6%)
  local copies, waits for them, and re-layouts  2.74 us (1%)
    all_gather x1, waiting for transfers between devices, collect_sources(): return jnp.sum(lax.all_gather(picked, 'chan'), axis=0)  107 us
    reduce_scatter x1, waiting for transfers between devices, body(): lax.psum_scatter(correlate(collected, chan_spec, factor), 'seg', scatter_...  69.6 us
    dot_general x5, matrix products, back_block(): jnp.einsum('sck,kl->scl', joined, inverse_table(block_index, factor), pre...  11.4 us
    select_n x5, other arithmetic, forward_table(): jnp.where(valid, jnp.cos(phase), 0.0)  6.77 us
    mul x1, other arithmetic, inverse_table(): weight * jnp.cos(phase)  5.32 us
  transfers between devices with their start and end apart: 3, of which 2 were waited for; matrix products, arithmetic and copies ran while one was open for 6% of the time, Pallas kernels for 0%

profile of v1, /device:TPU:16, one launch (start us, length us, event | category | flops | bytes accessed | tf_op | source)
XLA Modules:
  0.0 229.4 jit_solution(882237060225986424)
XLA Ops:
  6.5 0.9 slice.131
  7.4 1.7 collective-permute-start
  9.2 0.7 compare_and_fusion
  9.9 1.4 cosine_select_fusion.4
  11.3 1.4 cosine_select_fusion
  12.6 1.4 cosine_select_fusion.1
  14.0 1.4 cosine_select_fusion.2
  15.4 1.4 cosine_select_fusion.3
  16.7 0.8 fusion.177
  17.9 0.1 pad_maximum_fusion
  18.1 2.8 %convolution_bitcast_fusion = f32[5,4,8,128]{3,2,1,0:T(8,128)S(1)} fusion(f32[32,5,640]{2,0,1:T(8,128)S(1)} %fusion.156, f32[]{:T(128)} %fusion.177, s32[128]{0:T(128)S(1)} %iota_multiply_fusion), kind=kOutput, calls=%fused_computation.2 | convolution fusion | flops 161218560 | bytes 492036 | tf_op jit(solution)/shard_map/rbi,im->rbm/dot_general | solution.py:50
  20.9 0.4 fusion.19
  21.3 0.4 fusion.35
  21.8 0.4 fusion.31
  22.2 0.4 fusion.27
  22.6 0.4 fusion.23
  23.2 0.2 multiply_bitcast_fusion.1
  23.6 0.7 gather_fusion
  24.3 0.2 fusion.123
  24.5 0.7 copy.7
  25.3 5.3 %cosine_multiply_fusion = (f32[128,501]{0,1:T(8,128)S(1)}, f32[128,501]{0,1:T(8,128)S(1)}, f32[128,501]{0,1:T(8,128)S(1)}, f32[128,501]{0,1:T(8,128)S(1)}, f32[1...) fusion(s32[128]{0:T(128)S(1)} %iota_add_fusion.1, ...), kind=kLoop, calls=%fused_computation.165 | loop fusion | flops 3527040 | bytes 2574292 | tf_op jit(solution)/shard_map/mul | solution.py:70
  30.7 107.4 %all-gather.2.cloned.1.call-done = f32[32,32,2,640]{3,1,2,0:T(8,128)} async-done(((f32[1,32,2,640]{3,1,2,0:T(8,128)}), f32[32,32,2,640]{3,1,2,0:T(8,128)}) %all-gather.2.cloned.1.call-update) | async-done | bytes 5242896 | tf_op jit(solution)/shard_map/all_gather | solution.py:137
  138.1 2.8 %reduce_sum.29 = f32[32,2,640]{2,0,1:T(8,128)S(1)} reduce(f32[32,32,2,640]{3,1,2,0:T(8,128)} %all-gather.2.cloned.1.call-done, f32[]{:T(128)} %constant.121.clone.1), dimensions={0}, to_apply=%region_2.3 | reduce | flops 1269760 | bytes 5406724 | tf_op jit(solution)/shard_map/reduce_sum | solution.py:137
  140.9 0.2 multiply_add_fusion.4
  141.0 1.9 fusion
  142.9 0.3 multiply_add_fusion
  143.2 1.9 fusion.12
  145.1 0.2 multiply_add_fusion.2
  145.3 2.1 fusion.8
  147.4 1.9 fusion.4
  149.3 3.7 %add_add_fusion = f32[32,32,501]{2,1,0:T(8,128)} fusion(f32[32,32,501]{2,1,0:T(8,128)S(1)} %fusion.12, f32[32,32,501]{2,1,0:T(8,128)S(1)} %fusion.8, f32[32,32,501]{2,1,0:T(8,128)S(1)} %fusion, f32[32,32,501]{2,1,0:T(8,128)S(1)} %fusion.4, f32[32,32,128]{2,1,0:T(8,128)S(1)} %get-tuple-element.32, f32[32,32,128]{2,1,0:T(8,128)S(1)} %get-tuple-element.31, ...), kind=kOutput, calls=%fused_computation.1 | convolution fusion | flops 1578452224 | bytes 11822080 | tf_op jit(solution)/shard_map/sck,kl->scl/dot_general | solution.py:111
  153.0 69.6 %reduce-scatter.2.cloned.1.call-done = f32[2,32,501]{2,1,0:T(8,128)} async-done(((f32[32,32,501]{2,1,0:T(8,128)}), f32[2,32,501]{2,1,0:T(8,128)}) %reduce-scatter.2.cloned.1.call-update) | async-done | bytes 128272 | tf_op jit(solution)/shard_map/reduce_scatter | solution.py:155
  (43 shorter events, 0.9 us)
Async XLA Ops:
  6.5 11.0 %copy-start = (f32[32,2500]{1,0:T(8,128)S(1)}, f32[32,2500]{1,0:T(8,128)}, u32[]{:S(2)}) copy-start(f32[32,2500]{1,0:T(8,128)} %param.2) | copy-start | bytes 960004
  6.5 131.5 %all-gather.2.cloned.1.call-start = ((), (), s32[]{:S(2)}) async-start(), calls=%async_computation.1 | async-start | bytes 5406720 | tf_op jit(solution)/shard_map/all_gather | solution.py:137
  7.4 10.2 %collective-permute-start = (f32[32,60]{1,0:T(8,128)S(1)}, f32[32,60]{1,0:T(8,128)S(1)}, u32[]{:S(2)}, u32[]{:S(2)}) collective-permute-start(f32[32,60]{1,0:T(8,128)S(1)} %slice.131), channel_id=1, source_target_pairs={{0,1},{1,2},{2,3},{3,4},{4,5},{5,6},{6,7},{7,8},{8,9},{9,10},{10,1... | collective-permute-start | bytes 23048 | tf_op jit(solution)/shard_map/ppermute | solution.py:19
  25.2 197.4 %reduce-scatter.2.cloned.1.call-start = ((), (), s32[]{:S(2)}) async-start(), calls=%async_computation.2 | async-start | bytes 2228224 | tf_op jit(solution)/shard_map/reduce_scatter | solution.py:155
Sparse Core Ops, SparseCore 0:
  25.3 112.6 all-gather.1
  153.1 69.3 reduce-scatter.1
